TPU v7x, 512 devices: a whole 4x8x8 slice. The times are simulated.
512 devices in a mesh: row: 16 (over z, x_lo), col: 32 (over x_hi, y, core).
Axes of the slice: x: 4 (x_hi: 2, x_lo: 2; x = x_hi * 2 + x_lo), y: 8, z: 8, core: 2. Of those that a mesh axis runs over, the one named last changes fastest.
Arguments:
- tokens: bfloat16 [2048, 4096], P('row', 'col'), may hold values from -6 to 6
- upstream: bfloat16 [2048, 4096], P('row', 'col'), may hold values from -6 to 6
- w_in: bfloat16 [32, 16, 256, 256], P('col', 'row'), may hold values from -0.1875 to 0.1875
- in_codes: int32 [32, 16], P('col'), may hold values from -1 to 31, as said below
- w_out: bfloat16 [32, 16, 256, 256], P('col', 'row'), may hold values from -0.09375 to 0.09375
- out_codes: int32 [32, 16], P('col'), may hold values from -1 to 31, as said below
Outputs:
- layer_out: bfloat16 [2048, 4096], P('row', 'col')
- grad_tokens: bfloat16 [2048, 4096], P('row', 'col')
- grad_w_in: bfloat16 [32, 16, 256, 256], P('col', 'row')
- grad_w_out: bfloat16 [32, 16, 256, 256], P('col', 'row')
Inputs may be any that keep to these rules, and one draw needn't show every extreme that they name: `in_codes`: row c describes panel c's 16 slots: a code k names input tile row k // 2 and local hidden tile column k % 2; -1 marks an empty slot. Codes of a row are distinct, every row has one filled slot or more, and some row has all 16 slots filled. `out_codes`: row c describes panel c's 16 slots: a code k names output tile column k // 2 and local hidden tile row k % 2; -1 marks an empty slot. Codes of a row are distinct, every row has one filled slot or more, and some row has all 16 slots filled.
All inputs are finite; a program needn't handle non-finite values.
Results may differ from a plain program's by a relative error of at most 0.015.
Values may be sent and summed in bfloat16 or wider, within the bound.
A program may use at most 64 MiB of HBM per device.

v0:
```python
import jax
import jax.numpy as jnp
from jax import lax
from jax.sharding import PartitionSpec as P

D = 4096
FF = 16384


def silu_slope(hidden):
    sigmoid_value = jax.nn.sigmoid(hidden)
    return sigmoid_value * (1.0 + hidden * (1.0 - sigmoid_value))


def split_codes(slot_codes, tile_cols):
    filled = slot_codes >= 0
    clipped = jnp.maximum(slot_codes, 0)
    return (clipped // tile_cols, clipped % tile_cols, filled)


def selector(position, filled, classes):
    matches = position[:, None] == jnp.arange(classes, dtype=jnp.int32)[None, :]
    return (matches & filled[:, None]).astype(jnp.float32)


def slices_at(row_codes, col_codes, filled):
    return (row_codes, col_codes, filled)


def per_device(tokens, upstream, w_in, in_codes, w_out, out_codes):
    tile_size = w_in.shape[3]
    row_count = tokens.shape[0]
    tile_rows = D // tile_size
    tile_cols = FF // (tile_size * lax.axis_size("col"))
    own_slots = w_in.shape[1]
    highest = lax.Precision.HIGHEST
    in_row, in_col, in_filled = split_codes(in_codes[0], tile_cols)
    out_row, out_col, out_filled = split_codes(out_codes[0], tile_cols)
    first_slot = lax.axis_index("row") * own_slots
    whole_tokens, whole_upstream = (
        lax.all_gather(tokens, "col", axis=1, tiled=True),
        lax.all_gather(upstream, "col", axis=1, tiled=True),
    )
    token_tiles = whole_tokens.reshape(row_count, tile_rows, tile_size)
    up_tiles = whole_upstream.reshape(row_count, tile_rows, tile_size)
    slot_major_tokens = jnp.swapaxes(token_tiles, 0, 1)
    rows_at, cols_at, filled_at = slices_at(in_row, in_col, in_filled)
    picked = jnp.take(token_tiles, rows_at, axis=1)
    partial_sum = jnp.einsum(
        "tkd,kdn->tkn",
        picked,
        lax.all_gather(w_in, "row", axis=1, tiled=True)[0],
        preferred_element_type=jnp.float32,
    )
    hidden = jnp.einsum(
        "tkn,kj->tjn", partial_sum, selector(cols_at, filled_at, tile_cols), precision=highest
    )
    activ = jax.nn.silu(hidden).astype(jnp.bfloat16)
    rows_at, cols_at, filled_at = slices_at(out_row, out_col, out_filled)
    picked = jnp.take(activ, cols_at, axis=1)
    partial_sum = jnp.einsum(
        "tkf,kfd->tkd",
        picked,
        lax.all_gather(w_out, "row", axis=1, tiled=True)[0],
        preferred_element_type=jnp.float32,
    )
    layer_part = jnp.einsum(
        "tkd,ki->tid", partial_sum, selector(rows_at, filled_at, tile_rows), precision=highest
    )
    layer_out = lax.psum_scatter(
        layer_part.reshape(row_count, D).astype(jnp.bfloat16),
        "col",
        scatter_dimension=1,
        tiled=True,
    )
    rows_at, cols_at, filled_at = slices_at(out_row, out_col, out_filled)
    picked = jnp.take(up_tiles, rows_at, axis=1)
    partial_sum = jnp.einsum(
        "tkd,kfd->tkf",
        picked,
        lax.all_gather(w_out, "row", axis=1, tiled=True)[0],
        preferred_element_type=jnp.float32,
    )
    grad_activ = jnp.einsum(
        "tkf,kj->tjf", partial_sum, selector(cols_at, filled_at, tile_cols), precision=highest
    )
    grad_hidden = (grad_activ * silu_slope(hidden)).astype(jnp.bfloat16)
    grad_sends = jnp.take(jnp.swapaxes(grad_hidden, 0, 1), in_col, axis=0)
    activ_sends = jnp.take(jnp.swapaxes(activ, 0, 1), out_col, axis=0)
    upstream_sends = jnp.take(jnp.swapaxes(up_tiles, 0, 1), out_row, axis=0)
    token_sends = jnp.take(slot_major_tokens, in_row, axis=0)
    token_slots, grad_slots, activ_slots, upstream_slots = (
        lax.all_to_all(token_sends, "row", split_axis=0, concat_axis=1, tiled=True),
        lax.all_to_all(grad_sends, "row", split_axis=0, concat_axis=1, tiled=True),
        lax.all_to_all(activ_sends, "row", split_axis=0, concat_axis=1, tiled=True),
        lax.all_to_all(upstream_sends, "row", split_axis=0, concat_axis=1, tiled=True),
    )
    rows_at, cols_at, filled_at = slices_at(in_row, in_col, in_filled)
    picked = jnp.take(grad_hidden, cols_at, axis=1)
    partial_sum = jnp.einsum(
        "tkf,kdf->tkd",
        picked,
        lax.all_gather(w_in, "row", axis=1, tiled=True)[0],
        preferred_element_type=jnp.float32,
    )
    input_part = jnp.einsum(
        "tkd,ki->tid", partial_sum, selector(rows_at, filled_at, tile_rows), precision=highest
    )
    grad_tokens = lax.psum_scatter(
        input_part.reshape(row_count, D).astype(jnp.bfloat16),
        "col",
        scatter_dimension=1,
        tiled=True,
    )
    mine_in = lax.dynamic_slice_in_dim(in_filled, first_slot, own_slots)
    mine_out = lax.dynamic_slice_in_dim(out_filled, first_slot, own_slots)
    grad_w_in = jnp.einsum(
        "ktd,ktn->kdn", token_slots, grad_slots, preferred_element_type=jnp.float32
    )
    grad_w_in = jnp.where(mine_in[:, None, None], grad_w_in, 0.0).astype(jnp.bfloat16)[None]
    grad_w_out = jnp.einsum(
        "ktf,ktd->kfd", activ_slots, upstream_slots, preferred_element_type=jnp.float32
    )
    grad_w_out = jnp.where(mine_out[:, None, None], grad_w_out, 0.0).astype(jnp.bfloat16)[None]
    return (layer_out, grad_tokens, grad_w_in, grad_w_out)


def solution(mesh):
    placed = (
        P("row", "col"),
        P("row", "col"),
        P("col", "row", None, None),
        P("col", None),
        P("col", "row", None, None),
        P("col", None),
    )
    return jax.shard_map(
        per_device,
        mesh=mesh,
        in_specs=placed,
        out_specs=(
            P("row", "col"),
            P("row", "col"),
            P("col", "row", None, None),
            P("col", "row", None, None),
        ),
        check_vma=False,
    )
```

profile of v0, /device:TPU:16, one launch (start us, length us, event | category | flops | bytes accessed | tf_op | source)
XLA Modules:
  0.0 631.0 jit_solution(14606275297330410834)
XLA Ops:
  7.2 1.5 copy.59
  8.8 1.5 copy.52
  12.3 86.6 %all-gather.11.cloned.1.call-done = bf16[128,4096]{0,1:T(8,128)(2,1)} async-done(((bf16[128,128]{0,1:T(8,128)(2,1)}), bf16[128,4096]{0,1:T(8,128)(2,1)}) %all-gather.11.cloned.1.call-update) | async-done | bytes 1048592 | tf_op jit(solution)/shard_map/all_gather | solution.py:42
  98.9 1.5 copy.60
  102.1 7.5 %all-to-all-start.3 = ((bf16[16,128,256]{2,1,0:T(8,128)(2,1)}), bf16[16,128,256]{2,1,0:T(8,128)(2,1)}, u32[]{:S(2)}, u32[]{:S(2)}) async-start(bf16[16,128,256]{2,1,0:T(8,128)(2,1)} %broadcast_select_fusion.3), calls=%async_computation.3 | async-start | bytes 2097152 | tf_op jit(solution)/shard_map/all_to_all | solution.py:96
  110.8 72.0 %all-gather.5.cloned.1.call-done = bf16[128,4096]{0,1:T(8,128)(2,1)} async-done(((bf16[128,128]{0,1:T(8,128)(2,1)}), bf16[128,4096]{0,1:T(8,128)(2,1)}) %all-gather.5.cloned.1.call-update) | async-done | bytes 1048592 | tf_op jit(solution)/shard_map/all_gather | solution.py:41
  182.8 1.5 copy.53
  184.2 1.6 gather_fusion.4
  185.8 1.6 copy.65
  188.6 7.5 %all-to-all-start = ((bf16[16,128,256]{1,2,0:T(8,128)(2,1)}), bf16[16,128,256]{1,2,0:T(8,128)(2,1)}, u32[]{:S(2)}, u32[]{:S(2)}) async-start(bf16[16,128,256]{1,2,0:T(8,128)(2,1)} %broadcast_select_fusion.1), calls=%async_computation | async-start | bytes 2097152 | tf_op jit(solution)/shard_map/all_to_all | solution.py:93
  197.4 76.1 %all-gather.9.cloned.1.call-done = bf16[1,16,256,256]{3,2,0,1:T(8,128)(2,1)} async-done(((bf16[1,1,256,256]{3,2,0,1:T(8,128)(2,1)}), bf16[1,16,256,256]{3,2,0,1:T(8,128)(2,1)}) %all-gather.9.cloned.1.call-update) | async-done | bytes 2097168 | tf_op jit(solution)/shard_map/all_gather | solution.py:64
  273.5 2.4 fusion.25
  275.9 2.0 fusion.10
  277.9 69.6 %all-gather.7.cloned.1.call-done = bf16[1,16,256,256]{3,2,0,1:T(8,128)(2,1)} async-done(((bf16[1,1,256,256]{3,2,0,1:T(8,128)(2,1)}), bf16[1,16,256,256]{3,2,0,1:T(8,128)(2,1)}) %all-gather.7.cloned.1.call-update) | async-done | bytes 2097168 | tf_op jit(solution)/shard_map/all_gather | solution.py:52
  347.5 2.1 fusion.16
  349.7 2.0 fusion.14
  353.1 1.2 broadcast_select_fusion
  354.3 4.7 all-to-all-start.2
  360.6 2.3 fusion.37
  362.9 1.7 copy.76
  364.7 1.6 gather_fusion.3
  368.7 2.2 fusion.19
  370.9 8.0 %all-to-all-done.2 = bf16[16,128,256]{1,2,0:T(8,128)(2,1)} async-done(((bf16[16,128,256]{1,2,0:T(8,128)(2,1)}), bf16[16,128,256]{1,2,0:T(8,128)(2,1)}, u32[]{:S(2)}, u32[]{:S(2)}) %all-to-all-start.2) | async-done | bytes 1048608 | tf_op jit(solution)/shard_map/all_to_all | solution.py:95
  378.8 4.3 all-to-all-start.1
  383.3 2.3 fusion.34
  385.6 1.8 copy.77
  388.6 100.4 %reduce-scatter.7.cloned.1.call-done = bf16[128,128]{1,0:T(8,128)(2,1)} async-done(((bf16[4096,128]{1,0:T(8,128)(2,1)}), bf16[128,128]{1,0:T(8,128)(2,1)}) %reduce-scatter.7.cloned.1.call-update) | async-done | bytes 32784
  489.0 1.5 copy.73
  490.5 125.7 %reduce-scatter.9.cloned.1.call-done = bf16[128,128]{1,0:T(8,128)(2,1)} async-done(((bf16[4096,128]{1,0:T(8,128)(2,1)}), bf16[128,128]{1,0:T(8,128)(2,1)}) %reduce-scatter.9.cloned.1.call-update) | async-done | bytes 32784
  616.2 1.5 copy.75
  617.6 3.3 fusion.45
  620.9 3.2 fusion.44
  (74 shorter events, 13.9 us)
Async XLA Ops:
  7.2 91.7 %all-gather.11.cloned.1.call-start = ((), (), s32[]{:S(2)}) async-start(), calls=%async_computation.9 | async-start | bytes 1081344 | tf_op jit(solution)/shard_map/all_gather | solution.py:42
  8.7 174.0 %all-gather.5.cloned.1.call-start = ((), (), s32[]{:S(2)}) async-start(), calls=%async_computation.6 | async-start | bytes 1081344 | tf_op jit(solution)/shard_map/all_gather | solution.py:41
  10.3 263.2 %all-gather.9.cloned.1.call-start = ((), (), s32[]{:S(2)}) async-start(), calls=%async_computation.8 | async-start | bytes 2228224 | tf_op jit(solution)/shard_map/all_gather | solution.py:64
  11.0 336.5 %all-gather.7.cloned.1.call-start = ((), (), s32[]{:S(2)}) async-start(), calls=%async_computation.7 | async-start | bytes 2228224 | tf_op jit(solution)/shard_map/all_gather | solution.py:52
  12.2 88.7 %copy-start.4 = (s32[16]{0:T(128)}, s32[16]{0:T(128)S(1)}, u32[]{:S(2)}) copy-start(s32[16]{0:T(128)S(1)} %get-tuple-element.11) | copy-start | bytes 196
  101.0 8.7 %copy-start.12 = (s32[1,16]{1,0:T(1,128)S(1)}, s32[1,16]{1,0:T(1,128)}, u32[]{:S(2)}) copy-start(s32[1,16]{1,0:T(1,128)} %param.17) | copy-start | bytes 196
  101.0 9.3 %copy-start.13 = (s32[1,16]{1,0:T(1,128)S(1)}, s32[1,16]{1,0:T(1,128)}, u32[]{:S(2)}) copy-start(s32[1,16]{1,0:T(1,128)} %param.19) | copy-start | bytes 196
  102.1 86.5 %all-to-all-start.3 = ((bf16[16,128,256]{2,1,0:T(8,128)(2,1)}), bf16[16,128,256]{2,1,0:T(8,128)(2,1)}, u32[]{:S(2)}, u32[]{:S(2)}) async-start(bf16[16,128,256]{2,1,0:T(8,128)(2,1)} %broadcast_select_fusion.3), calls=%async_computation.3 | async-start | bytes 2097152 | tf_op jit(solution)/shard_map/all_to_all | solution.py:96
  109.7 239.9 %copy-start.10 = (s32[16]{0:T(128)}, s32[16]{0:T(128)S(1)}, u32[]{:S(2)}) copy-start(s32[16]{0:T(128)S(1)} %get-tuple-element.9) | copy-start | bytes 196
  110.3 239.4 %copy-start.6 = (pred[16]{0:T(512)(128)(4,1)}, pred[16]{0:T(512)(128)(4,1)S(1)}, u32[]{:S(2)}) copy-start(pred[16]{0:T(512)(128)(4,1)S(1)} %get-tuple-element.23) | copy-start | bytes 52
  110.8 165.1 %copy-start.8 = (pred[16]{0:T(512)(128)(4,1)}, pred[16]{0:T(512)(128)(4,1)S(1)}, u32[]{:S(2)}) copy-start(pred[16]{0:T(512)(128)(4,1)S(1)} %get-tuple-element.21) | copy-start | bytes 52
  188.6 165.7 %all-to-all-start = ((bf16[16,128,256]{1,2,0:T(8,128)(2,1)}), bf16[16,128,256]{1,2,0:T(8,128)(2,1)}, u32[]{:S(2)}, u32[]{:S(2)}) async-start(bf16[16,128,256]{1,2,0:T(8,128)(2,1)} %broadcast_select_fusion.1), calls=%async_computation | async-start | bytes 2097152 | tf_op jit(solution)/shard_map/all_to_all | solution.py:93
  354.3 5.7 copy-start.1
  354.3 24.5 %all-to-all-start.2 = ((bf16[16,128,256]{1,2,0:T(8,128)(2,1)}), bf16[16,128,256]{1,2,0:T(8,128)(2,1)}, u32[]{:S(2)}, u32[]{:S(2)}) async-start(bf16[16,128,256]{1,2,0:T(8,128)(2,1)} %broadcast_select_fusion), calls=%async_computation.2 | async-start | bytes 2097152 | tf_op jit(solution)/shard_map/all_to_all | solution.py:95
  359.0 130.0 %reduce-scatter.7.cloned.1.call-start = ((), (), s32[]{:S(2)}) async-start(), calls=%async_computation.10 | async-start | bytes 1081344
  360.0 0.7 copy-start.5
  360.0 0.6 copy-start.9
  362.9 1.8 copy-start.11
  366.3 1.8 copy-start
  366.9 1.7 copy-start.3
  368.6 14.6 %copy-start.7 = (pred[16]{0:T(512)(128)(4,1)S(1)}, pred[16]{0:T(512)(128)(4,1)}, u32[]{:S(2)}) copy-start(pred[16]{0:T(512)(128)(4,1)} %copy-done.6) | copy-start | bytes 52
  370.9 12.4 %copy-start.2 = (f32[128,16,256]{2,0,1:T(8,128)S(1)}, f32[128,16,256]{2,0,1:T(8,128)}, u32[]{:S(2)}) copy-start(f32[128,16,256]{2,0,1:T(8,128)} %fusion.19) | copy-start | bytes 6291460
  378.8 242.1 %all-to-all-start.1 = ((bf16[16,128,256]{2,1,0:T(8,128)(2,1)}), bf16[16,128,256]{2,1,0:T(8,128)(2,1)}, u32[]{:S(2)}, u32[]{:S(2)}) async-start(bf16[16,128,256]{2,1,0:T(8,128)(2,1)} %broadcast_select_fusion.2), calls=%async_computation.1 | async-start | bytes 2097152 | tf_op jit(solution)/shard_map/all_to_all | solution.py:94
  383.2 233.0 %reduce-scatter.9.cloned.1.call-start = ((), (), s32[]{:S(2)}) async-start(), calls=%async_computation.11 | async-start | bytes 1081344
  385.6 1.8 copy-start.14
  385.6 2.4 copy-start.15
Sparse Core Ops, SparseCore 0:
  11.9 86.8 all-gather.10
  102.8 79.9 all-gather.4
  184.8 88.6 all-gather.8
  275.4 72.0 all-gather.6
  364.8 124.1 reduce-scatter.6
  494.2 121.9 reduce-scatter.8
where the time goes:
time: 632 us; the launch traced here: 631 us
  waiting for transfers between devices  540 us (85%)
  starting transfers between devices  24.5 us (4%)
  local copies, waits for them, and re-layouts  23.4 us (4%)
  matrix products  22.3 us (4%)
  between operations  14.5 us (2%)
  other arithmetic  6.7 us (1%)
    unnamed x8, waiting for transfers between devices  227 us
    all_gather x1, waiting for transfers between devices, per_device(): lax.all_gather(upstream, 'col', axis=1, tiled=True)  86.6 us
    all_gather x1, waiting for transfers between devices, per_device(): lax.all_gather(w_out, 'row', axis=1, tiled=True)[0]  76.1 us
    all_gather x1, waiting for transfers between devices, per_device(): lax.all_gather(tokens, 'col', axis=1, tiled=True)  72 us
    all_gather x1, waiting for transfers between devices, per_device(): lax.all_gather(w_in, 'row', axis=1, tiled=True)[0]  69.6 us
  transfers between devices with their start and end apart: 10, of which 7 were waited for; matrix products, arithmetic and copies ran while one was open for 7% of the time, Pallas kernels for 0%

commit v1 on v0

--- a/solution.py
+++ b/solution.py
@@ -38,7 +38,9 @@
     out_row, out_col, out_filled = split_codes(out_codes[0], tile_cols)
     first_slot = lax.axis_index("row") * own_slots
     whole_tokens, whole_upstream = (
-        lax.all_gather(tokens, "col", axis=1, tiled=True),
+        jnp.concatenate(
+            lax.all_to_all(jnp.stack([tokens] * lax.axis_size("col")), "col", 0, 0), axis=1
+        ),
         lax.all_gather(upstream, "col", axis=1, tiled=True),
     )
     token_tiles = whole_tokens.reshape(row_count, tile_rows, tile_size)

time: 632 us -> 555 us (0.88)
  waiting for transfers between devices: 540 us -> 447 us
  starting transfers between devices: 24.5 us -> 42.9 us
    all_gather x1 -> x0, waiting for transfers between devices: 72 us -> none  [per_device(): lax.all_gather(tokens, 'col', axis=1, tiled=True)]
    all_gather x1, waiting for transfers between devices: 86.6 us -> 37.2 us  [per_device(): lax.all_gather(upstream, 'col', axis=1, tiled=True)]
    all_to_all x0 -> x1, waiting for transfers between devices: none -> 28.2 us  [per_device(): lax.all_to_all(jnp.stack([tokens] * lax.axis_size('col')), 'col', 0, 0)]
    all_to_all x0 -> x1, starting transfers between devices: none -> 10.1 us  [per_device(): lax.all_to_all(jnp.stack([tokens] * lax.axis_size('col')), 'col', 0, 0)]
    unnamed x8 -> x7, waiting for transfers between devices: 227 us -> 227 us
  transfers between devices with their start and end apart: 10 -> 10, of which waited for: 7 -> 7; matrix products, arithmetic and copies ran while one was open for 7% -> 8% of each run, Pallas kernels for 0% -> 0%
where the time goes in v1:
time: 555 us; the launch traced here: 554 us
  waiting for transfers between devices  447 us (81%)
  starting transfers between devices  42.9 us (8%)
  matrix products  22.3 us (4%)
  local copies, waits for them, and re-layouts  21.2 us (4%)
  between operations  14.2 us (3%)
  other arithmetic  6.03 us (1%)
    unnamed x7, waiting for transfers between devices  227 us
    all_gather x1, waiting for transfers between devices, per_device(): lax.all_gather(w_out, 'row', axis=1, tiled=True)[0]  76.7 us
    all_gather x1, waiting for transfers between devices, per_device(): lax.all_gather(w_in, 'row', axis=1, tiled=True)[0]  69.6 us
    all_gather x1, waiting for transfers between devices, per_device(): lax.all_gather(upstream, 'col', axis=1, tiled=True)  37.2 us
    all_to_all x1, waiting for transfers between devices, per_device(): lax.all_to_all(jnp.stack([tokens] * lax.axis_size('col')), 'col', 0, 0)  28.2 us
    all_to_all x1, starting transfers between devices, per_device(): lax.all_to_all(upstream_sends, 'row', split_axis=0, concat_axis=1, tiled=...  12.8 us
  transfers between devices with their start and end apart: 10, of which 7 were waited for; matrix products, arithmetic and copies ran while one was open for 8% of the time, Pallas kernels for 0%

profile of v1, /device:TPU:16, one launch (start us, length us, event | category | flops | bytes accessed | tf_op | source)
XLA Modules:
  0.0 553.8 jit_solution(8638579956523846494)
XLA Ops:
  7.2 1.5 copy.62
  10.3 1.3 stack.2
  11.6 10.1 %all-to-all-start = ((bf16[32,128,128]{1,2,0:T(8,128)(2,1)}), bf16[32,128,128]{1,2,0:T(8,128)(2,1)S(1)}, u32[]{:S(2)}, u32[]{:S(2)}) async-start(bf16[32,128,128]{1,2,0:T(8,128)(2,1)} %stack.2), calls=%async_computation | async-start | bytes 2097152 | tf_op jit(solution)/shard_map/all_to_all | solution.py:42
  22.5 28.2 %all-to-all-done = bf16[32,128,128]{1,2,0:T(8,128)(2,1)S(1)} async-done(((bf16[32,128,128]{1,2,0:T(8,128)(2,1)}), bf16[32,128,128]{1,2,0:T(8,128)(2,1)S(1)}, u32[]{:S(2)}, u32[]{:S(2)}) %all-to-all-start) | async-done | bytes 1048608 | tf_op jit(solution)/shard_map/all_to_all | solution.py:42
  53.6 10.7 %all-to-all-start.1 = ((bf16[16,128,256]{1,2,0:T(8,128)(2,1)}), bf16[16,128,256]{1,2,0:T(8,128)(2,1)}, u32[]{:S(2)}, u32[]{:S(2)}) async-start(bf16[16,128,256]{1,2,0:T(8,128)(2,1)} %broadcast_select_fusion.1), calls=%async_computation.1 | async-start | bytes 2097152 | tf_op jit(solution)/shard_map/all_to_all | solution.py:95
  65.5 37.2 %all-gather.8.cloned.1.call-done = bf16[128,4096]{0,1:T(8,128)(2,1)} async-done(((bf16[128,128]{0,1:T(8,128)(2,1)}), bf16[128,4096]{0,1:T(8,128)(2,1)}) %all-gather.8.cloned.1.call-update) | async-done | bytes 1048592 | tf_op jit(solution)/shard_map/all_gather | solution.py:44
  102.6 1.5 copy.63
  104.8 1.1 broadcast_select_fusion.3
  105.9 12.8 %all-to-all-start.4 = ((bf16[16,128,256]{2,1,0:T(8,128)(2,1)}), bf16[16,128,256]{2,1,0:T(8,128)(2,1)}, u32[]{:S(2)}, u32[]{:S(2)}) async-start(bf16[16,128,256]{2,1,0:T(8,128)(2,1)} %broadcast_select_fusion.3), calls=%async_computation.4 | async-start | bytes 2097152 | tf_op jit(solution)/shard_map/all_to_all | solution.py:98
  119.9 76.7 %all-gather.6.cloned.1.call-done = bf16[1,16,256,256]{3,2,0,1:T(8,128)(2,1)} async-done(((bf16[1,1,256,256]{3,2,0,1:T(8,128)(2,1)}), bf16[1,16,256,256]{3,2,0,1:T(8,128)(2,1)}) %all-gather.6.cloned.1.call-update) | async-done | bytes 2097168 | tf_op jit(solution)/shard_map/all_gather | solution.py:66
  196.7 2.4 fusion.25
  199.1 2.0 fusion.10
  201.1 69.6 %all-gather.4.cloned.1.call-done = bf16[1,16,256,256]{3,2,0,1:T(8,128)(2,1)} async-done(((bf16[1,1,256,256]{3,2,0,1:T(8,128)(2,1)}), bf16[1,16,256,256]{3,2,0,1:T(8,128)(2,1)}) %all-gather.4.cloned.1.call-update) | async-done | bytes 2097168 | tf_op jit(solution)/shard_map/all_gather | solution.py:54
  270.7 2.1 fusion.16
  272.8 2.0 fusion.14
  276.2 1.3 broadcast_select_fusion
  277.5 4.7 all-to-all-start.3
  283.8 2.3 fusion.37
  286.1 1.7 copy.79
  287.9 1.6 gather_fusion.3
  290.1 1.2 broadcast_select_fusion.2
  291.8 2.2 fusion.19
  294.1 8.0 %all-to-all-done.3 = bf16[16,128,256]{1,2,0:T(8,128)(2,1)} async-done(((bf16[16,128,256]{1,2,0:T(8,128)(2,1)}), bf16[16,128,256]{1,2,0:T(8,128)(2,1)}, u32[]{:S(2)}, u32[]{:S(2)}) %all-to-all-start.3) | async-done | bytes 1048608 | tf_op jit(solution)/shard_map/all_to_all | solution.py:97
  302.0 4.3 all-to-all-start.2
  306.4 2.3 fusion.34
  308.8 1.7 copy.80
  311.8 100.5 %reduce-scatter.7.cloned.1.call-done = bf16[128,128]{1,0:T(8,128)(2,1)} async-done(((bf16[4096,128]{1,0:T(8,128)(2,1)}), bf16[128,128]{1,0:T(8,128)(2,1)}) %reduce-scatter.7.cloned.1.call-update) | async-done | bytes 32784
  412.2 1.5 copy.76
  413.7 125.5 %reduce-scatter.9.cloned.1.call-done = bf16[128,128]{1,0:T(8,128)(2,1)} async-done(((bf16[4096,128]{1,0:T(8,128)(2,1)}), bf16[128,128]{1,0:T(8,128)(2,1)}) %reduce-scatter.9.cloned.1.call-update) | async-done | bytes 32784
  539.2 1.5 copy.78
  540.7 3.3 fusion.45
  544.0 3.3 fusion.44
  (74 shorter events, 13.8 us)
Async XLA Ops:
  7.2 15.2 %copy-start.12 = (s32[1,16]{1,0:T(1,128)S(1)}, s32[1,16]{1,0:T(1,128)}, u32[]{:S(2)}) copy-start(s32[1,16]{1,0:T(1,128)} %param.17) | copy-start | bytes 196
  7.2 95.5 %all-gather.8.cloned.1.call-start = ((), (), s32[]{:S(2)}) async-start(), calls=%async_computation.9 | async-start | bytes 1081344 | tf_op jit(solution)/shard_map/all_gather | solution.py:44
  8.7 188.0 %all-gather.6.cloned.1.call-start = ((), (), s32[]{:S(2)}) async-start(), calls=%async_computation.8 | async-start | bytes 2228224 | tf_op jit(solution)/shard_map/all_gather | solution.py:66
  11.6 39.1 %all-to-all-start = ((bf16[32,128,128]{1,2,0:T(8,128)(2,1)}), bf16[32,128,128]{1,2,0:T(8,128)(2,1)S(1)}, u32[]{:S(2)}, u32[]{:S(2)}) async-start(bf16[32,128,128]{1,2,0:T(8,128)(2,1)} %stack.2), calls=%async_computation | async-start | bytes 2097152 | tf_op jit(solution)/shard_map/all_to_all | solution.py:42
  21.7 249.1 %all-gather.4.cloned.1.call-start = ((), (), s32[]{:S(2)}) async-start(), calls=%async_computation.7 | async-start | bytes 2228224 | tf_op jit(solution)/shard_map/all_gather | solution.py:54
  22.4 250.4 %copy-start.10 = (s32[16]{0:T(128)}, s32[16]{0:T(128)S(1)}, u32[]{:S(2)}) copy-start(s32[16]{0:T(128)S(1)} %get-tuple-element.9) | copy-start | bytes 196
  52.5 11.9 %copy-start.13 = (s32[1,16]{1,0:T(1,128)S(1)}, s32[1,16]{1,0:T(1,128)}, u32[]{:S(2)}) copy-start(s32[1,16]{1,0:T(1,128)} %param.19) | copy-start | bytes 196
  53.6 52.3 %all-to-all-start.1 = ((bf16[16,128,256]{1,2,0:T(8,128)(2,1)}), bf16[16,128,256]{1,2,0:T(8,128)(2,1)}, u32[]{:S(2)}, u32[]{:S(2)}) async-start(bf16[16,128,256]{1,2,0:T(8,128)(2,1)} %broadcast_select_fusion.1), calls=%async_computation.1 | async-start | bytes 2097152 | tf_op jit(solution)/shard_map/all_to_all | solution.py:95
  64.4 40.3 %copy-start.4 = (s32[16]{0:T(128)}, s32[16]{0:T(128)S(1)}, u32[]{:S(2)}) copy-start(s32[16]{0:T(128)S(1)} %get-tuple-element.11) | copy-start | bytes 196
  65.0 207.9 %copy-start.6 = (pred[16]{0:T(512)(128)(4,1)}, pred[16]{0:T(512)(128)(4,1)S(1)}, u32[]{:S(2)}) copy-start(pred[16]{0:T(512)(128)(4,1)S(1)} %get-tuple-element.23) | copy-start | bytes 52
  65.5 133.6 %copy-start.8 = (pred[16]{0:T(512)(128)(4,1)}, pred[16]{0:T(512)(128)(4,1)S(1)}, u32[]{:S(2)}) copy-start(pred[16]{0:T(512)(128)(4,1)S(1)} %get-tuple-element.21) | copy-start | bytes 52
  105.9 171.6 %all-to-all-start.4 = ((bf16[16,128,256]{2,1,0:T(8,128)(2,1)}), bf16[16,128,256]{2,1,0:T(8,128)(2,1)}, u32[]{:S(2)}, u32[]{:S(2)}) async-start(bf16[16,128,256]{2,1,0:T(8,128)(2,1)} %broadcast_select_fusion.3), calls=%async_computation.4 | async-start | bytes 2097152 | tf_op jit(solution)/shard_map/all_to_all | solution.py:98
  277.5 5.7 %copy-start.1 = (bf16[1,16,256,256]{3,2,0,1:T(8,128)(2,1)S(1)}, bf16[1,16,256,256]{3,2,0,1:T(8,128)(2,1)}, u32[]{:S(2)}) copy-start(bf16[1,16,256,256]{3,2,0,1:T(8,128)(2,1)} %all-gather.6.cloned.1.call-done) | copy-start | bytes 6291460
  277.5 24.5 %all-to-all-start.3 = ((bf16[16,128,256]{1,2,0:T(8,128)(2,1)}), bf16[16,128,256]{1,2,0:T(8,128)(2,1)}, u32[]{:S(2)}, u32[]{:S(2)}) async-start(bf16[16,128,256]{1,2,0:T(8,128)(2,1)} %broadcast_select_fusion), calls=%async_computation.3 | async-start | bytes 2097152 | tf_op jit(solution)/shard_map/all_to_all | solution.py:97
  282.2 130.1 %reduce-scatter.7.cloned.1.call-start = ((), (), s32[]{:S(2)}) async-start(), calls=%async_computation.10 | async-start | bytes 1081344
  283.2 0.7 copy-start.5
  283.2 0.6 copy-start.9
  286.1 1.8 copy-start.11
  289.5 1.8 copy-start
  290.1 1.7 copy-start.3
  291.8 14.6 %copy-start.7 = (pred[16]{0:T(512)(128)(4,1)S(1)}, pred[16]{0:T(512)(128)(4,1)}, u32[]{:S(2)}) copy-start(pred[16]{0:T(512)(128)(4,1)} %copy-done.6) | copy-start | bytes 52
  294.1 12.4 %copy-start.2 = (f32[128,16,256]{2,0,1:T(8,128)S(1)}, f32[128,16,256]{2,0,1:T(8,128)}, u32[]{:S(2)}) copy-start(f32[128,16,256]{2,0,1:T(8,128)} %fusion.19) | copy-start | bytes 6291460
  302.0 242.0 %all-to-all-start.2 = ((bf16[16,128,256]{2,1,0:T(8,128)(2,1)}), bf16[16,128,256]{2,1,0:T(8,128)(2,1)}, u32[]{:S(2)}, u32[]{:S(2)}) async-start(bf16[16,128,256]{2,1,0:T(8,128)(2,1)} %broadcast_select_fusion.2), calls=%async_computation.2 | async-start | bytes 2097152 | tf_op jit(solution)/shard_map/all_to_all | solution.py:96
  306.4 232.9 %reduce-scatter.9.cloned.1.call-start = ((), (), s32[]{:S(2)}) async-start(), calls=%async_computation.11 | async-start | bytes 1081344
  308.8 1.8 copy-start.14
  308.8 2.4 copy-start.15
Sparse Core Ops, SparseCore 0:
  11.9 90.6 all-gather.7
  104.7 91.9 all-gather.5
  198.8 71.9 all-gather.3
  288.0 124.1 reduce-scatter.6
  417.4 121.7 reduce-scatter.8
